TPU v7x, 128 devices: a whole 4x4x4 slice. The times are simulated.
128 devices in a mesh: row: 8 (over x, y_hi), col: 16 (over y_lo, z, core).
Axes of the slice: x: 4, y: 4 (y_hi: 2, y_lo: 2; y = y_hi * 2 + y_lo), z: 4, core: 2. Of those that a mesh axis runs over, the one named last changes fastest.
Arguments:
- train_inputs: bfloat16 [512, 8192], P(('row', 'col')), may hold values from -6 to 6
- train_grads: bfloat16 [512, 8192], P(('row', 'col')), may hold values from -6 to 6
- query_inputs: bfloat16 [256, 8192], P(('row', 'col')), may hold values from -6 to 6
- query_grads: bfloat16 [256, 8192], P(('row', 'col')), may hold values from -6 to 6
- input_basis: bfloat16 [8192, 8192], P('row', 'col'), may hold values from -0.0625 to 0.0625
- output_basis: bfloat16 [8192, 8192], P('col', 'row'), may hold values from -0.0625 to 0.0625
- eigenvalues: float32 [8192, 8192], P('row', 'col'), may hold values from 0.5 to 5
- query_starts: int32 [16], replicated, may hold values from 0 to 255, as said below
- query_ends: int32 [16], replicated, may hold values from 1 to 256, as said below
Outputs:
- scores: float32 [16, 512], replicated
Inputs may be any that keep to these rules, and one draw needn't show every extreme that they name: Query q covers the query rows query_starts[q] <= r < query_ends[q]: a nonempty span of at most 128 rows that lies inside one aligned block of 128 rows (rows k * 128 to (k + 1) * 128 - 1); spans of different queries may intersect or share a block. `query_ends`: see query_starts.
All inputs are finite; a program needn't handle non-finite values.
Results may differ from a plain program's by a relative error of at most 0.005.
Values may be sent and summed in bfloat16 or wider, within the bound.
A program may use at most 64 MiB of HBM per device.

v0:
```python
import math
import jax
import jax.numpy as jnp
from jax import lax
from jax.sharding import Mesh
from jax.sharding import PartitionSpec as P

D_IN = 8192
D_OUT = 8192
QBLOCK = 128
COL = ("col_0", "col_1", "col_2")
ROW = ("row_0", "row_1")
ROW_COL = ("row_0", "row_1", "col_0", "col_1", "col_2")
damping = 0.1


def laid_out(parts, dim):
    parts = jnp.moveaxis(parts, 0, dim)
    dims = parts.shape
    return parts.reshape(*dims[:dim], dims[dim] * dims[dim + 1], *dims[dim + 2 :])


def gather_together(arrays, axis, dims):
    line = jnp.concatenate([a.reshape(-1) for a in arrays])
    lines, at, gathered = (lax.all_gather(line, axis), 0, [])
    for a, dim in zip(arrays, dims):
        parts = lines[:, at : at + a.size].reshape(-1, *a.shape)
        gathered.append(laid_out(parts, dim))
        at += a.size
    return tuple(gathered)


def by_axis(value, axes):
    for axis in axes:
        value = lax.psum(value, axis)
    return value


def shards(
    train_inputs,
    train_grads,
    query_inputs,
    query_grads,
    input_basis,
    output_basis,
    eigenvalues,
    query_starts,
    query_ends,
):
    grouped = gather_together((train_inputs, query_inputs), COL, (0, 0))
    train_in, query_in = (
        lax.all_to_all(grouped[0], ROW, split_axis=1, concat_axis=0, tiled=True),
        lax.all_to_all(grouped[1], ROW, split_axis=1, concat_axis=0, tiled=True),
    )
    spread = (
        lax.all_to_all(train_grads, COL, split_axis=1, concat_axis=0, tiled=True),
        lax.all_to_all(query_grads, COL, split_axis=1, concat_axis=0, tiled=True),
    )
    train_out, query_out = gather_together((spread[0], spread[1]), ROW, (0, 0))
    train_in_part = jnp.dot(train_in, input_basis, preferred_element_type=jnp.float32)
    query_in_part = jnp.dot(query_in, input_basis, preferred_element_type=jnp.float32)
    train_out_part = jnp.dot(train_out, output_basis, preferred_element_type=jnp.float32)
    query_out_part = jnp.dot(query_out, output_basis, preferred_element_type=jnp.float32)
    in_sums = lax.psum((train_in_part, query_in_part), ROW)
    out_sums = lax.psum((train_out_part, query_out_part), COL)
    train_in_rot = in_sums[0].astype(jnp.bfloat16)
    query_in_rot = in_sums[1].astype(jnp.bfloat16)
    train_grad_rot = out_sums[0].astype(jnp.bfloat16)
    query_grad_rot = out_sums[1].astype(jnp.bfloat16)
    grads_wide = train_grad_rot.astype(jnp.float32)
    denominator = eigenvalues + damping

    def per_query(span):
        span_start, span_end = span
        block_top = span_start // QBLOCK * QBLOCK
        grad_rows = lax.dynamic_slice_in_dim(query_grad_rot, block_top, QBLOCK, 0)
        input_rows = lax.dynamic_slice_in_dim(query_in_rot, block_top, QBLOCK, 0)
        positions = block_top + jnp.arange(QBLOCK, dtype=jnp.int32)
        inside = (positions >= span_start) & (positions < span_end)
        grad_rows = jnp.where(inside[:, None], grad_rows, jnp.zeros((), grad_rows.dtype))
        outer_sum = lax.dot_general(
            grad_rows, input_rows, (((0,), (0,)), ((), ())), preferred_element_type=jnp.float32
        )
        scaled = (outer_sum / denominator).astype(jnp.bfloat16)
        paired = lax.dot_general(
            train_in_rot, scaled, (((1,), (1,)), ((), ())), preferred_element_type=jnp.float32
        )
        return jnp.sum(grads_wide * paired, axis=1)

    partial_scores = lax.map(per_query, (query_starts, query_ends))
    totals = by_axis(partial_scores, ROW_COL)
    return totals * (1.0 / math.sqrt(D_IN * D_OUT * QBLOCK))


def solution(mesh):
    split = Mesh(mesh.devices.reshape(4, 2, 2, 4, 2), ("row_0", "row_1", "col_0", "col_1", "col_2"))
    placed = (
        P(ROW_COL, None),
        P(ROW_COL, None),
        P(ROW_COL, None),
        P(ROW_COL, None),
        P(ROW, COL),
        P(COL, ROW),
        P(ROW, COL),
        P(),
        P(),
    )
    return jax.shard_map(shards, mesh=split, in_specs=placed, out_specs=P(), check_vma=False)
```

profile of v0, /device:TPU:1, one launch (start us, length us, event | category | flops | bytes accessed | tf_op | source)
XLA Modules:
  0.0 458.6 jit_solution(13673715249605043826)
XLA Ops:
  6.5 0.9 copy.26
  7.5 0.8 copy.27
  8.2 0.6 pad_maximum_fusion.1
  8.9 13.6 %all_to_all.70 = bf16[2,16,512]{2,0,1:T(2,128)(2,1)S(1)} all-to-all(bf16[2,16,512]{2,0,1:T(2,128)(2,1)} %bitcast.54), channel_id=1, replica_groups=mesh['row_0'=4,'row_1'=2,'col_0'=2,'col_1'=4,'col_2'=2] {'col_0','col_1'..., dimensions={1} | all-to-all | bytes 65536 | tf_op jit(solution)/shard_map/all_to_all | solution.py:57
  22.6 3.7 all-to-all-start
  26.2 3.2 broadcast_add_fusion
  29.5 2.7 all-to-all-done
  32.2 31.4 %all-gather = bf16[393216]{0:T(1024)(128)(2,1)S(1)} all-gather(bf16[49152]{0:T(1024)(128)(2,1)S(1)} %pad_maximum_fusion), channel_id=2, replica_groups=mesh['row_0'=4,'row_1'=2,'col_0'=2,'col_1'=4,'col_2'=2] {'row_0','row_1'}, dimensions={0}, use_global_device_ids=true | all-gather | bytes 884736 | tf_op jit(solution)/shard_map/all_gather | solution.py:25
  64.0 1.0 reshape_reshape.9
  65.0 1.8 reshape.40
  66.9 0.9 slice.17
  67.7 1.3 all_to_all.58
  69.0 1.1 copy.21
  70.1 4.5 all-to-all-start.2
  74.7 1.8 fusion.18
  76.4 0.8 reshape_reshape.8
  77.3 2.5 fusion.15
  79.7 1.1 slice.18
  80.8 2.3 all_to_all.62
  83.1 2.8 copy.22
  85.9 6.6 %all-to-all-start.3 = ((bf16[64,8,1024]{2,0,1:T(8,128)(2,1)}), bf16[64,8,1024]{2,0,1:T(8,128)(2,1)}, u32[]{:S(2)}, u32[]{:S(2)}) async-start(bf16[64,8,1024]{2,0,1:T(8,128)(2,1)} %copy.22), calls=%async_computation.3 | async-start | bytes 2097152 | tf_op jit(solution)/shard_map/all_to_all | solution.py:52
  92.6 74.4 %all-reduce.4 = (bf16[256,1024]{1,0:T(8,128)(2,1)}, bf16[512,1024]{1,0:T(8,128)(2,1)}) all-reduce(f32[256,1024]{1,0:T(8,128)} %fusion.15, f32[512,1024]{1,0:T(8,128)S(1)} %fusion.18), channel_id=1, replica_groups=mesh['row_0'=4,'row_1'=2,'col_0'=2,'col_1'=4,'col_2'=2] {'col_0','col_1'..., use_global_device_ids=true, to_apply=%region_0.0 | all-reduce | flops 786432 | bytes 4718592 | tf_op jit(solution)/shard_map/psum | solution.py:65
  166.9 1.5 copy.23
  168.4 2.6 fusion.16
  171.0 3.3 fusion.17
  174.3 81.4 %all-reduce.5 = (bf16[256,512]{1,0:T(8,128)(2,1)}, bf16[512,512]{1,0:T(8,128)(2,1)}) all-reduce(f32[256,512]{1,0:T(8,128)} %fusion.16, f32[512,512]{1,0:T(8,128)} %fusion.17), channel_id=1, replica_groups=mesh['row_0'=4,'row_1'=2,'col_0'=2,'col_1'=4,'col_2'=2] {'row_0','row_1'}, use_global_device_ids=true, to_apply=%region_1.0 | all-reduce | flops 393216 | bytes 2359296 | tf_op jit(solution)/shard_map/psum | solution.py:64
  255.7 127.2 %while.12 = (s32[]{:T(128)}, f32[16,512]{1,0:T(8,128)S(1)}, s32[16]{0:T(128)S(1)}, s32[16]{0:T(128)S(1)}, bf16[256,1024]{1,0:T(8,128)(2,1)}, /*index=5*/bf16[256...) while((s32[]{:T(128)}, f32[16,512]{1,0:T(8,128)S(1)}, ...), condition=%wide.region_6.7_spmd, body=%wide.region_4.6_spmd.sunk | while | flops 673316864 | bytes 5119617 | solution.py:90
  259.4 1.2 compare_and_fusion.2
  260.6 2.9 fusion.35
  267.4 1.2 compare_and_fusion.2
  268.6 2.9 fusion.35
  275.3 1.2 compare_and_fusion.2
  276.6 2.9 fusion.35
  283.3 1.2 compare_and_fusion.2
  284.5 2.9 fusion.35
  291.2 1.2 compare_and_fusion.2
  292.5 2.9 fusion.35
  299.2 1.2 compare_and_fusion.2
  300.4 2.9 fusion.35
  307.1 1.2 compare_and_fusion.2
  308.4 2.9 fusion.35
  315.1 1.2 compare_and_fusion.2
  316.3 2.9 fusion.35
  323.0 1.2 compare_and_fusion.2
  324.3 2.9 fusion.35
  331.0 1.2 compare_and_fusion.2
  332.2 2.9 fusion.35
  338.9 1.2 compare_and_fusion.2
  340.2 2.9 fusion.35
  346.9 1.2 compare_and_fusion.2
  348.1 2.9 fusion.35
  354.9 1.2 compare_and_fusion.2
  356.1 2.9 fusion.35
  362.8 1.2 compare_and_fusion.2
  364.0 2.9 fusion.35
  370.8 1.2 compare_and_fusion.2
  372.0 2.9 fusion.35
  378.7 1.2 compare_and_fusion.2
  380.0 2.9 fusion.35
  383.0 11.8 %psum.67 = f32[16,512]{1,0:T(8,128)S(1)} all-reduce(f32[16,512]{1,0:T(8,128)S(1)} %get-tuple-element.119), channel_id=1, replica_groups=mesh['row_0'=4,'row_1'=2,'col_0'=2,'col_1'=4,'col_2'=2] {'row_0'}, use_global_device_ids=true, to_apply=%region_7.8 | all-reduce | flops 8192 | bytes 65536 | tf_op jit(solution)/shard_map/psum | solution.py:35
  394.8 7.5 %psum.68 = f32[16,512]{1,0:T(8,128)S(1)} all-reduce(f32[16,512]{1,0:T(8,128)S(1)} %psum.67), channel_id=1, replica_groups=mesh['row_0'=4,'row_1'=2,'col_0'=2,'col_1'=4,'col_2'=2] {'row_1'}, use_global_device_ids=true, to_apply=%region_8.9 | all-reduce | flops 8192 | bytes 65536 | tf_op jit(solution)/shard_map/psum | solution.py:35
  402.3 6.6 %psum.69 = f32[16,512]{1,0:T(8,128)S(1)} all-reduce(f32[16,512]{1,0:T(8,128)S(1)} %psum.68), channel_id=1, replica_groups=mesh['row_0'=4,'row_1'=2,'col_0'=2,'col_1'=4,'col_2'=2] {'col_0'}, use_global_device_ids=true, to_apply=%region_9.10 | all-reduce | flops 8192 | bytes 65536 | tf_op jit(solution)/shard_map/psum | solution.py:35
  409.0 18.8 %psum.70 = f32[16,512]{1,0:T(8,128)S(1)} all-reduce(f32[16,512]{1,0:T(8,128)S(1)} %psum.69), channel_id=1, replica_groups=mesh['row_0'=4,'row_1'=2,'col_0'=2,'col_1'=4,'col_2'=2] {'col_1'}, use_global_device_ids=true, to_apply=%region_10.11 | all-reduce | flops 8192 | bytes 65536 | tf_op jit(solution)/shard_map/psum | solution.py:35
  427.7 23.4 %psum.71 = f32[16,512]{1,0:T(8,128)S(1)} all-reduce(f32[16,512]{1,0:T(8,128)S(1)} %psum.70), channel_id=1, replica_groups=mesh['row_0'=4,'row_1'=2,'col_0'=2,'col_1'=4,'col_2'=2] {'col_2'}, use_global_device_ids=true, to_apply=%region_11.12 | all-reduce | flops 8192 | bytes 65536 | tf_op jit(solution)/shard_map/psum | solution.py:35
  (74 shorter events, 21.5 us)
Async XLA Ops:
  6.5 68.1 %copy-start = (bf16[512,1024]{1,0:T(8,128)(2,1)S(1)}, bf16[512,1024]{1,0:T(8,128)(2,1)}, u32[]{:S(2)}) copy-start(bf16[512,1024]{1,0:T(8,128)(2,1)} %param.16) | copy-start | bytes 3145732
  6.5 58.5 %all-gather.4.cloned.1.call-start = ((), (), s32[]{:S(2)}) async-start(), calls=%async_computation.4 | async-start | bytes 1671168 | tf_op jit(solution)/shard_map/all_gather | solution.py:25
  22.6 9.6 %all-to-all-start = ((bf16[4,16,512]{2,0,1:T(4,128)(2,1)}), bf16[4,16,512]{2,0,1:T(4,128)(2,1)S(1)}, u32[]{:S(2)}, u32[]{:S(2)}) async-start(bf16[4,16,512]{2,0,1:T(4,128)(2,1)} %bitcast.51), calls=%async_computation | async-start | bytes 131072 | tf_op jit(solution)/shard_map/all_to_all | solution.py:56
  63.9 1.1 copy-start.3
  66.8 3.3 copy-start.1
  70.1 6.3 %slice-start = ((bf16[8,49152]{1,0:T(8,128)(2,1)}), bf16[8,16384]{1,0:T(8,128)(2,1)S(1)}, s32[]{:S(2)}) async-start(bf16[8,49152]{1,0:T(8,128)(2,1)} %copy-done.3), calls=%async_computation.5 | async-start | bytes 524288 | tf_op jit(solution)/shard_map/slice | solution.py:27
  70.1 15.8 %all-to-all-start.2 = ((bf16[32,8,1024]{2,0,1:T(8,128)(2,1)}), bf16[32,8,1024]{2,0,1:T(8,128)(2,1)}, u32[]{:S(2)}, u32[]{:S(2)}) async-start(bf16[32,8,1024]{2,0,1:T(8,128)(2,1)} %copy.21), calls=%async_computation.2 | async-start | bytes 1048576 | tf_op jit(solution)/shard_map/all_to_all | solution.py:53
  77.2 2.5 copy-start.2
  85.9 85.1 %all-to-all-start.3 = ((bf16[64,8,1024]{2,0,1:T(8,128)(2,1)}), bf16[64,8,1024]{2,0,1:T(8,128)(2,1)}, u32[]{:S(2)}, u32[]{:S(2)}) async-start(bf16[64,8,1024]{2,0,1:T(8,128)(2,1)} %copy.22), calls=%async_computation.3 | async-start | bytes 2097152 | tf_op jit(solution)/shard_map/all_to_all | solution.py:52
  171.0 84.7 %copy-start.4 = (s32[16]{0:T(128)S(1)}, s32[16]{0:T(128)}, u32[]{:S(2)}) copy-start(s32[16]{0:T(128)} %param.18) | copy-start | bytes 196
  171.0 84.7 %copy-start.5 = (s32[16]{0:T(128)S(1)}, s32[16]{0:T(128)}, u32[]{:S(2)}) copy-start(s32[16]{0:T(128)} %param.19) | copy-start | bytes 196
Sparse Core Ops, SparseCore 0:
  9.1 38.4 all-gather.3
where the time goes:
time: 461 us; the launch traced here: 459 us
  blocking collectives  269 us (58%)
  matrix products  56.8 us (12%)
  loops' own time  40.5 us (9%)
  local copies, waits for them, and re-layouts  37.2 us (8%)
  other arithmetic  24.1 us (5%)
  starting transfers between devices  14.8 us (3%)
  between operations  13.5 us (3%)
    psum x1, blocking collectives, shards(): in_sums = lax.psum((train_in_part, query_in_part), ROW)  81.4 us
    psum x1, blocking collectives, shards(): out_sums = lax.psum((train_out_part, query_out_part), COL)  74.4 us
    psum x5, blocking collectives, by_axis(): value = lax.psum(value, axis)  68.1 us
    dot_general x16, matrix products, per_query(): lax.dot_general(train_in_rot, scaled, (((1,), (1,)), ((), ())), preferred...  46.7 us
    another operation x1, loops' own time, shards(): partial_scores = lax.map(per_query, (query_starts, query_ends))  40.5 us
    all_gather x1, blocking collectives, gather_together(): lines, at, gathered = (lax.all_gather(line, axis), 0, [])  31.4 us
    and x16, other arithmetic, per_query(): inside = (positions >= span_start) & (positions < span_end)  19.6 us
    dynamic_slice x32, local copies, waits for them, and re-layouts, shards(): partial_scores = lax.map(per_query, (query_starts, query_ends))  19.4 us
  transfers between devices with their start and end apart: 4, of which 1 were waited for; matrix products, arithmetic and copies ran while one was open for 4% of the time, Pallas kernels for 0%

commit v1 on v0

--- a/solution.py
+++ b/solution.py
@@ -61,7 +61,7 @@
     query_in_part = jnp.dot(query_in, input_basis, preferred_element_type=jnp.float32)
     train_out_part = jnp.dot(train_out, output_basis, preferred_element_type=jnp.float32)
     query_out_part = jnp.dot(query_out, output_basis, preferred_element_type=jnp.float32)
-    in_sums = lax.psum((train_in_part, query_in_part), ROW)
+    in_sums = lax.psum(lax.psum((train_in_part, query_in_part), "row_0"), "row_1")
     out_sums = lax.psum((train_out_part, query_out_part), COL)
     train_in_rot = in_sums[0].astype(jnp.bfloat16)
     query_in_rot = in_sums[1].astype(jnp.bfloat16)

time: 461 us -> 433 us (0.939)
  blocking collectives: 269 us -> 224 us
  waiting for transfers between devices: 2.68 us -> 23.1 us
    psum x1, blocking collectives: 81.4 us -> 37.6 us  [shards(): lax.psum(lax.psum((train_in_part, query_in_part), 'row_0'), 'row_1')]
    all_gather x1, waiting for transfers between devices: 0.01 us -> 19.8 us  [gather_together(): lines, at, gathered = (lax.all_gather(line, axis), 0, [])]
    all_gather x1, blocking collectives: 31.4 us -> 39.5 us  [gather_together(): lines, at, gathered = (lax.all_gather(line, axis), 0, [])]
    psum x5, blocking collectives: 68.1 us -> 62.4 us  [by_axis(): value = lax.psum(value, axis)]
  transfers between devices with their start and end apart: 4 -> 5, of which waited for: 1 -> 2; matrix products, arithmetic and copies ran while one was open for 4% -> 5% of each run, Pallas kernels for 0% -> 0%
where the time goes in v1:
time: 433 us; the launch traced here: 431 us
  blocking collectives  224 us (52%)
  matrix products  56.6 us (13%)
  loops' own time  40.5 us (9%)
  local copies, waits for them, and re-layouts  35.1 us (8%)
  other arithmetic  24.1 us (6%)
  waiting for transfers between devices  23.1 us (5%)
  starting transfers between devices  14.1 us (3%)
  between operations  13.6 us (3%)
    psum x1, blocking collectives, shards(): out_sums = lax.psum((train_out_part, query_out_part), COL)  70.5 us
    psum x5, blocking collectives, by_axis(): value = lax.psum(value, axis)  62.4 us
    dot_general x16, matrix products, per_query(): lax.dot_general(train_in_rot, scaled, (((1,), (1,)), ((), ())), preferred...  46.7 us
    another operation x1, loops' own time, shards(): partial_scores = lax.map(per_query, (query_starts, query_ends))  40.5 us
    all_gather x1, blocking collectives, gather_together(): lines, at, gathered = (lax.all_gather(line, axis), 0, [])  39.5 us
    psum x1, blocking collectives, shards(): lax.psum(lax.psum((train_in_part, query_in_part), 'row_0'), 'row_1')  37.6 us
    all_gather x1, waiting for transfers between devices, gather_together(): lines, at, gathered = (lax.all_gather(line, axis), 0, [])  19.8 us
    and x16, other arithmetic, per_query(): inside = (positions >= span_start) & (positions < span_end)  19.6 us
  transfers between devices with their start and end apart: 5, of which 2 were waited for; matrix products, arithmetic and copies ran while one was open for 5% of the time, Pallas kernels for 0%

profile of v1, /device:TPU:1, one launch (start us, length us, event | category | flops | bytes accessed | tf_op | source)
XLA Modules:
  0.0 430.6 jit_solution(11037794049871127775)
XLA Ops:
  6.5 0.9 copy.26
  7.5 0.8 copy.27
  8.9 13.6 %all_to_all.70 = bf16[2,16,512]{2,0,1:T(2,128)(2,1)S(1)} all-to-all(bf16[2,16,512]{2,0,1:T(2,128)(2,1)} %bitcast.55), channel_id=1, replica_groups=mesh['row_0'=4,'row_1'=2,'col_0'=2,'col_1'=4,'col_2'=2] {'col_0','col_1'..., dimensions={1} | all-to-all | bytes 65536 | tf_op jit(solution)/shard_map/all_to_all | solution.py:57
  22.6 3.7 all-to-all-start
  26.2 19.8 %all-gather.4.cloned.1.call-done = bf16[786432]{0:T(1024)(128)(2,1)} async-done(((bf16[49152]{0:T(1024)(128)(2,1)}), bf16[786432]{0:T(1024)(128)(2,1)}) %all-gather.4.cloned.1.call-update) | async-done | bytes 1572880 | tf_op jit(solution)/shard_map/all_gather | solution.py:25
  46.1 1.8 reshape.40
  47.9 0.8 slice.17
  48.7 1.3 all_to_all.58
  50.0 1.1 copy.21
  51.1 6.1 %all-to-all-start.2 = ((bf16[32,8,1024]{2,0,1:T(8,128)(2,1)}), bf16[32,8,1024]{2,0,1:T(8,128)(2,1)S(1)}, u32[]{:S(2)}, u32[]{:S(2)}) async-start(bf16[32,8,1024]{2,0,1:T(8,128)(2,1)} %copy.21), calls=%async_computation.2 | async-start | bytes 1048576 | tf_op jit(solution)/shard_map/all_to_all | solution.py:53
  57.2 3.2 broadcast_add_fusion
  60.5 1.1 slice.18
  61.5 1.6 all_to_all.62
  63.1 1.6 copy.22
  64.6 3.3 all-to-all-done.2
  67.9 4.2 all-to-all-start.3
  72.2 39.5 %all-gather = bf16[393216]{0:T(1024)(128)(2,1)S(1)} all-gather(bf16[49152]{0:T(1024)(128)(2,1)S(1)} %pad_maximum_fusion), channel_id=2, replica_groups=mesh['row_0'=4,'row_1'=2,'col_0'=2,'col_1'=4,'col_2'=2] {'row_0','row_1'}, dimensions={0}, use_global_device_ids=true | all-gather | bytes 884736 | tf_op jit(solution)/shard_map/all_gather | solution.py:25
  112.1 1.0 reshape_reshape.9
  113.2 2.4 fusion.16
  115.6 3.2 fusion.17
  118.9 1.8 fusion.18
  120.7 0.8 reshape_reshape.8
  121.5 2.4 fusion.15
  123.9 70.5 %all-reduce.9 = (bf16[256,1024]{1,0:T(8,128)(2,1)}, bf16[512,1024]{1,0:T(8,128)(2,1)}) all-reduce(f32[256,1024]{1,0:T(8,128)} %fusion.15, f32[512,1024]{1,0:T(8,128)S(1)} %fusion.18), channel_id=1, replica_groups=mesh['row_0'=4,'row_1'=2,'col_0'=2,'col_1'=4,'col_2'=2] {'col_0','col_1'..., use_global_device_ids=true, to_apply=%region_0.0 | all-reduce | flops 786432 | bytes 4718592 | tf_op jit(solution)/shard_map/psum | solution.py:65
  194.3 1.5 copy.23
  195.9 37.6 %all-reduce.8 = (bf16[256,512]{1,0:T(8,128)(2,1)}, bf16[512,512]{1,0:T(8,128)(2,1)}) all-reduce(f32[256,512]{1,0:T(8,128)} %get-tuple-element.176, f32[512,512]{1,0:T(8,128)} %get-tuple-element.177), channel_id=1, replica_groups=mesh['row_0'=4,'row_1'=2,'col_0'=2,'col_1'=4,'col_2'=2] {'row_1'}, use_global_device_ids=true, to_apply=%region_2.0 | all-reduce | flops 393216 | bytes 2359296 | tf_op jit(solution)/shard_map/psum | solution.py:64
  233.5 127.2 %while.12 = (s32[]{:T(128)}, f32[16,512]{1,0:T(8,128)S(1)}, s32[16]{0:T(128)S(1)}, s32[16]{0:T(128)S(1)}, bf16[256,1024]{1,0:T(8,128)(2,1)}, /*index=5*/bf16[256...) while((s32[]{:T(128)}, f32[16,512]{1,0:T(8,128)S(1)}, ...), condition=%wide.region_8.9_spmd, body=%wide.region_6.8_spmd.sunk | while | flops 673316864 | bytes 5119617 | solution.py:90
  237.2 1.2 compare_and_fusion.2
  238.4 2.9 fusion.35
  245.1 1.2 compare_and_fusion.2
  246.4 2.9 fusion.35
  253.1 1.2 compare_and_fusion.2
  254.3 2.9 fusion.35
  261.0 1.2 compare_and_fusion.2
  262.3 2.9 fusion.35
  269.0 1.2 compare_and_fusion.2
  270.2 2.9 fusion.35
  276.9 1.2 compare_and_fusion.2
  278.2 2.9 fusion.35
  284.9 1.2 compare_and_fusion.2
  286.1 2.9 fusion.35
  292.8 1.2 compare_and_fusion.2
  294.1 2.9 fusion.35
  300.8 1.2 compare_and_fusion.2
  302.0 2.9 fusion.35
  308.8 1.2 compare_and_fusion.2
  310.0 2.9 fusion.35
  316.7 1.2 compare_and_fusion.2
  318.0 2.9 fusion.35
  324.7 1.2 compare_and_fusion.2
  325.9 2.9 fusion.35
  332.6 1.2 compare_and_fusion.2
  333.9 2.9 fusion.35
  340.6 1.2 compare_and_fusion.2
  341.8 2.9 fusion.35
  348.5 1.2 compare_and_fusion.2
  349.8 2.9 fusion.35
  356.5 1.2 compare_and_fusion.2
  357.7 2.9 fusion.35
  360.7 11.2 %psum.83 = f32[16,512]{1,0:T(8,128)S(1)} all-reduce(f32[16,512]{1,0:T(8,128)S(1)} %get-tuple-element.119), channel_id=1, replica_groups=mesh['row_0'=4,'row_1'=2,'col_0'=2,'col_1'=4,'col_2'=2] {'row_0'}, use_global_device_ids=true, to_apply=%region_9.10 | all-reduce | flops 8192 | bytes 65536 | tf_op jit(solution)/shard_map/psum | solution.py:35
  371.9 6.7 %psum.84 = f32[16,512]{1,0:T(8,128)S(1)} all-reduce(f32[16,512]{1,0:T(8,128)S(1)} %psum.83), channel_id=1, replica_groups=mesh['row_0'=4,'row_1'=2,'col_0'=2,'col_1'=4,'col_2'=2] {'row_1'}, use_global_device_ids=true, to_apply=%region_10.11 | all-reduce | flops 8192 | bytes 65536 | tf_op jit(solution)/shard_map/psum | solution.py:35
  378.6 5.8 %psum.85 = f32[16,512]{1,0:T(8,128)S(1)} all-reduce(f32[16,512]{1,0:T(8,128)S(1)} %psum.84), channel_id=1, replica_groups=mesh['row_0'=4,'row_1'=2,'col_0'=2,'col_1'=4,'col_2'=2] {'col_0'}, use_global_device_ids=true, to_apply=%region_11.12 | all-reduce | flops 8192 | bytes 65536 | tf_op jit(solution)/shard_map/psum | solution.py:35
  384.5 23.9 %psum.86 = f32[16,512]{1,0:T(8,128)S(1)} all-reduce(f32[16,512]{1,0:T(8,128)S(1)} %psum.85), channel_id=1, replica_groups=mesh['row_0'=4,'row_1'=2,'col_0'=2,'col_1'=4,'col_2'=2] {'col_1'}, use_global_device_ids=true, to_apply=%region_12.13 | all-reduce | flops 8192 | bytes 65536 | tf_op jit(solution)/shard_map/psum | solution.py:35
  408.3 14.8 %psum.87 = f32[16,512]{1,0:T(8,128)S(1)} all-reduce(f32[16,512]{1,0:T(8,128)S(1)} %psum.86), channel_id=1, replica_groups=mesh['row_0'=4,'row_1'=2,'col_0'=2,'col_1'=4,'col_2'=2] {'col_2'}, use_global_device_ids=true, to_apply=%region_13.14 | all-reduce | flops 8192 | bytes 65536 | tf_op jit(solution)/shard_map/psum | solution.py:35
  (73 shorter events, 22.2 us)
Async XLA Ops:
  6.5 112.3 %copy-start = (bf16[512,1024]{1,0:T(8,128)(2,1)S(1)}, bf16[512,1024]{1,0:T(8,128)(2,1)}, u32[]{:S(2)}) copy-start(bf16[512,1024]{1,0:T(8,128)(2,1)} %param.16) | copy-start | bytes 3145732
  6.5 39.5 %all-gather.4.cloned.1.call-start = ((), (), s32[]{:S(2)}) async-start(), calls=%async_computation.4 | async-start | bytes 1671168 | tf_op jit(solution)/shard_map/all_gather | solution.py:25
  22.6 28.5 %all-to-all-start = ((bf16[4,16,512]{2,0,1:T(4,128)(2,1)}), bf16[4,16,512]{2,0,1:T(4,128)(2,1)S(1)}, u32[]{:S(2)}, u32[]{:S(2)}) async-start(bf16[4,16,512]{2,0,1:T(4,128)(2,1)} %bitcast.52), calls=%async_computation | async-start | bytes 131072 | tf_op jit(solution)/shard_map/all_to_all | solution.py:56
  51.1 16.8 %all-to-all-start.2 = ((bf16[32,8,1024]{2,0,1:T(8,128)(2,1)}), bf16[32,8,1024]{2,0,1:T(8,128)(2,1)S(1)}, u32[]{:S(2)}, u32[]{:S(2)}) async-start(bf16[32,8,1024]{2,0,1:T(8,128)(2,1)} %copy.21), calls=%async_computation.2 | async-start | bytes 1048576 | tf_op jit(solution)/shard_map/all_to_all | solution.py:53
  67.9 47.7 %all-to-all-start.3 = ((bf16[64,8,1024]{2,0,1:T(8,128)(2,1)}), bf16[64,8,1024]{2,0,1:T(8,128)(2,1)}, u32[]{:S(2)}, u32[]{:S(2)}) async-start(bf16[64,8,1024]{2,0,1:T(8,128)(2,1)} %copy.22), calls=%async_computation.3 | async-start | bytes 2097152 | tf_op jit(solution)/shard_map/all_to_all | solution.py:52
  72.1 123.7 %all-reduce.7.cloned.1.call-start = ((), (), s32[]{:S(2)}) async-start(), calls=%async_computation.5 | async-start | bytes 3145728 | tf_op jit(solution)/shard_map/psum | solution.py:64
  112.1 3.5 copy-start.1
  118.9 1.8 slice-start
  194.3 39.1 %copy-start.2 = (s32[16]{0:T(128)S(1)}, s32[16]{0:T(128)}, u32[]{:S(2)}) copy-start(s32[16]{0:T(128)} %param.18) | copy-start | bytes 196
  194.3 39.1 %copy-start.3 = (s32[16]{0:T(128)S(1)}, s32[16]{0:T(128)}, u32[]{:S(2)}) copy-start(s32[16]{0:T(128)} %param.19) | copy-start | bytes 196
Sparse Core Ops, SparseCore 0:
  9.1 36.9 all-gather.3
  119.0 52.5 all-reduce.6
